TPU v7x, 128 devices: a whole 4x4x4 slice. The times are simulated.
128 devices in a mesh: mem: 16 (over z, x), sub: 8 (over y, core).
Axes of the slice: x: 4, y: 4, z: 4, core: 2. Of those that a mesh axis runs over, the one named last changes fastest.
Arguments:
- ensemble: float32 [64, 3, 256, 2048], P('mem', None, 'sub'), may hold values from -6 to 6
- sea_depth: float32 [256, 2048], P('sub'), may hold values from 0.5 to 2
- cutoff: int32 [256, 2048], P('sub', 'mem'), may hold values from 16 to 64
- obs_index: int32 [4, 256], replicated, may hold values from 0 to 524287
- obs_value: float32 [4, 256], replicated, may hold values from -6 to 6
- obs_var: float32 [4, 256], replicated, may hold values from 0.5 to 2
Outputs:
- analysis: float32 [64, 3, 256, 2048], P(None, None, 'sub', 'mem')
All inputs are finite; a program needn't handle non-finite values.
Results may differ from a plain program's by a relative error of at most 0.0001.
Values sent between devices are 32-bit elements; how exact they have to be, the bound alone decides.
A program may use at most 192 MiB of HBM per device.

v0:
```python
import jax
import jax.numpy as jnp
from jax import lax
from jax.sharding import PartitionSpec as P

STEPS = 4
BATCHES = 4
step_size = 0.3
coriolis = 0.2
highest = lax.Precision.HIGHEST


def padded(shard, sides, width):
    for axis, dim in sides:
        peers, length = (lax.axis_size(axis), shard.shape[dim])
        up = [(i, (i + 1) % peers) for i in range(peers)]
        down = [(j, i) for i, j in up]
        last = lax.slice_in_dim(shard, length - width, length, axis=dim)
        leading = lax.slice_in_dim(shard, 0, width, axis=dim)
        before = lax.ppermute(last, axis, up)
        after = lax.ppermute(leading, axis, down)
        shard = jnp.concatenate([before, shard, after], axis=dim)
    return shard


def across_cols(field):
    return (jnp.roll(field, -1, 2) - jnp.roll(field, 1, 2)) * 0.5


def momentum(height, east_wind, north_wind):
    height_ext = padded(height, (("sub", 1),), 1)
    height_dx = (height_ext[:, 2:] - height_ext[:, :-2]) * 0.5
    east_new = east_wind + step_size * (coriolis * north_wind - height_dx)
    north_new = north_wind + step_size * (-coriolis * east_wind - across_cols(height))
    return (east_new, north_new)


def continuity(height, east_wind, north_wind, sea_depth):
    flux_ext = padded(sea_depth * east_wind, (("sub", 1),), 1)
    divergence = (flux_ext[:, 2:] - flux_ext[:, :-2]) * 0.5 + across_cols(sea_depth * north_wind)
    return height - step_size * divergence


def localize(obs_x, obs_y, cell_x, cell_y, radius_sq, size_x, size_y):
    gap_x = jnp.abs(cell_x[None, :] - obs_x[:, None])
    gap_x = jnp.minimum(gap_x, size_x - gap_x)
    gap_y = jnp.abs(cell_y[None, :] - obs_y[:, None])
    gap_y = jnp.minimum(gap_y, size_y - gap_y)
    dist_sq = (gap_x * gap_x + gap_y * gap_y).astype(jnp.float32)
    dist_ratio = dist_sq / radius_sq[None, :]
    return jnp.square(jnp.maximum(1.0 - dist_ratio, 0.0))


def analysis_weights(prior_obs, values, variance):
    member_count = prior_obs.shape[1]
    obs_mean = jnp.mean(prior_obs, 1)
    obs_anom = prior_obs - obs_mean[:, None]
    innov_cov = jnp.dot(obs_anom, obs_anom.T, precision=highest) / (member_count - 1) + jnp.diag(
        variance
    )
    factor = jnp.linalg.cholesky(innov_cov)
    right_side = jnp.concatenate([(values - obs_mean)[:, None], obs_anom], 1)
    solved = jax.scipy.linalg.cho_solve((factor, True), right_side)
    return (obs_anom, solved[:, :1] - 0.5 * solved[:, 1:])


def update_state(members, obs_anom, weights_mix, loc_weight, cell_count):
    member_count = members.shape[0]
    obs_count = obs_anom.shape[0]
    state_anom = members - jnp.mean(members, 0)
    cross_cov = jnp.dot(obs_anom, state_anom, precision=highest) / (member_count - 1)
    loc_gain = (cross_cov.reshape(obs_count, 3, cell_count) * loc_weight[:, None, :]).reshape(
        obs_count, 3 * cell_count
    )
    return members + jnp.dot(weights_mix.T, loc_gain, precision=highest)


def local(ensemble, sea_depth, cutoff, obs_index, obs_value, obs_var):
    height = ensemble[:, 0]
    east_wind = ensemble[:, 1]
    north_wind = ensemble[:, 2]
    for step_id in range(STEPS - 1):
        east_wind, north_wind = momentum(height, east_wind, north_wind)
        height = continuity(height, east_wind, north_wind, sea_depth)
    east_wind, north_wind = momentum(height, east_wind, north_wind)
    height = continuity(height, east_wind, north_wind, sea_depth)
    point_state = lax.all_to_all(
        jnp.stack([height, east_wind, north_wind], 1),
        "mem",
        split_axis=3,
        concat_axis=0,
        tiled=True,
    )
    member_count = point_state.shape[0]
    row_count, col_block = cutoff.shape
    x_start = lax.axis_index("sub") * row_count
    y_start = lax.axis_index("mem") * col_block
    size_x = row_count * lax.axis_size("sub")
    size_y = col_block * lax.axis_size("mem")
    cell_count = row_count * col_block
    cell_ids = jnp.arange(cell_count, dtype=jnp.int32)
    cell_x = x_start + cell_ids // col_block
    cell_y = y_start + cell_ids % col_block
    radius_sq = jnp.square(cutoff.reshape(cell_count).astype(jnp.float32))
    members = point_state.reshape(member_count, 3 * cell_count)
    for batch_id in range(BATCHES):
        obs_cell = obs_index[batch_id]
        obs_x = obs_cell // size_y
        obs_y = obs_cell % size_y
        select_obs_x = obs_cell // size_y
        select_obs_y = obs_cell % size_y
        inside = (
            (select_obs_x >= x_start)
            & (select_obs_x < x_start + row_count)
            & (select_obs_y >= y_start)
            & (select_obs_y < y_start + col_block)
        )
        local_id = (select_obs_x - x_start) * col_block + (select_obs_y - y_start)
        local_part = lax.dot_general(
            ((local_id[:, None] == cell_ids[None, :]) & inside[:, None]).astype(jnp.float32),
            members[:, :cell_count],
            (((1,), (1,)), ((), ())),
            precision=highest,
        )
        prior_obs = lax.psum(local_part, ("mem", "sub"))
        obs_anom, weights_mix = analysis_weights(prior_obs, obs_value[batch_id], obs_var[batch_id])
        loc_weight = localize(obs_x, obs_y, cell_x, cell_y, radius_sq, size_x, size_y)
        members = update_state(members, obs_anom, weights_mix, loc_weight, cell_count)
    return members.reshape(member_count, 3, row_count, col_block)


def solution(mesh):
    return jax.shard_map(
        local,
        mesh=mesh,
        in_specs=(P("mem", None, "sub", None), P("sub", None), P("sub", "mem"), P(), P(), P()),
        out_specs=P(None, None, "sub", "mem"),
        check_vma=False,
    )
```

profile of v0, /device:TPU:1, one launch (start us, length us, event | category | flops | bytes accessed | tf_op | source)
XLA Modules:
  0.0 1229.5 jit_solution(545508524932749431)
XLA Ops:
  83.5 15.4 %reshape.856 = f32[16,1,49152]{2,1,0:T(1,128)} reshape(f32[2048,3,4,32]{3,2,1,0:T(4,128)} %bitcast.231) | data formatting | bytes 6291456
  106.8 14.0 %fusion.34 = (f32[256,4096]{0,1:T(8,128)}, f32[256,4096]{0,1:T(8,128)}, f32[256,4096]{0,1:T(8,128)}, f32[256,4096]{0,1:T(8,128)S(1)}) fusion(s32[256]{0:T(256)S(1)} %copy-done.18, s32[256]{0:T(256)S(1)} %copy-done.17, f32[4096]{0:T(1024)S(1)} %multiply_bitcast_fusion, s32[4096]{0:T(1024)S(1)} %copy-done.16, s32[4096]{0:T(1024)S(1)} %copy-done.15, ...), kind=kLoop, calls=%fused_computation.58 | loop fusion | flops 67108864 | bytes 16834560 | tf_op jit(solution)/shard_map/square | solution.py:51
  126.4 12.6 %copy.123 = f32[256,12288]{1,0:T(8,128)} copy(f32[256,12288]{0,1:T(8,128)} %bitcast.227) | data formatting | bytes 25165824 | tf_op jit(solution)/shard_map/mul | solution.py:72
  146.8 12.6 %copy.126 = f32[256,12288]{1,0:T(8,128)} copy(f32[256,12288]{0,1:T(8,128)} %bitcast.228) | data formatting | bytes 25165824 | tf_op jit(solution)/shard_map/mul | solution.py:72
  167.2 12.6 %copy.129 = f32[256,12288]{1,0:T(8,128)} copy(f32[256,12288]{0,1:T(8,128)} %bitcast.229) | data formatting | bytes 25165824 | tf_op jit(solution)/shard_map/mul | solution.py:72
  187.5 12.8 %copy.132 = f32[256,12288]{1,0:T(8,128)} copy(f32[256,12288]{0,1:T(8,128)} %bitcast.230) | data formatting | bytes 25165824 | tf_op jit(solution)/shard_map/mul | solution.py:72
  214.1 15.0 %reshape.857 = f32[2048,3,4,32]{3,2,1,0:T(4,128)} reshape(f32[16,49152]{1,0:T(8,128)} %reduce.9) | data formatting | bytes 6291456
  247.5 141.1 %all-reduce.6.cloned.1.call-done = f32[256,64]{0,1:T(8,128)} async-done(((f32[256,64]{0,1:T(8,128)}), f32[256,64]{0,1:T(8,128)}) %all-reduce.6.cloned.1.call-update) | async-done | bytes 65552 | tf_op jit(solution)/shard_map/psum | solution.py:125
  419.7 12.5 %cholesky.231 = f32[128,128]{1,0:T(8,128)S(1)} custom-call(f32[128,128]{1,0:T(8,128)} %convolution_subtract_fusion.3), custom_call_target="Cholesky" | custom-call | tf_op jit(solution)/shard_map/jit(cholesky)/cholesky | solution.py:61
  442.7 21.1 %custom-call.20 = f32[2,128,128]{1,2,0:T(8,128)} custom-call(f32[2,128,128]{2,1,0:T(8,128)} %get-tuple-element.33), custom_call_target="InvertDiagBlocksLowerTriangular" | custom-call | tf_op jit(solution)/shard_map/jit(_cho_solve)/triangular_solve | solution.py:63
  469.3 13.6 %fusion.3 = f32[256,12288]{1,0:T(8,128)S(1)} fusion(f32[256,12288]{1,0:T(8,128)} %copy.123, f32[256,64]{0,1:T(8,128)S(1)} %broadcast_subtract_fusion.3, f32[64,12288]{1,0:T(8,128)S(1)} %reshape.826, f32[12288]{0:T(1024)} %bitcast.240), kind=kOutput, calls=%fused_computation.15 | convolution fusion | flops 2422996992 | bytes 28426240 | tf_op jit(solution)/shard_map/dot_general | solution.py:71
  496.6 135.9 %all-reduce.8.cloned.1.call-done = f32[256,64]{0,1:T(8,128)} async-done(((f32[256,64]{0,1:T(8,128)}), f32[256,64]{0,1:T(8,128)}) %all-reduce.8.cloned.1.call-update) | async-done | bytes 65552 | tf_op jit(solution)/shard_map/psum | solution.py:125
  663.0 12.5 %cholesky.265 = f32[128,128]{1,0:T(8,128)S(1)} custom-call(f32[128,128]{1,0:T(8,128)} %convolution_subtract_fusion.2), custom_call_target="Cholesky" | custom-call | tf_op jit(solution)/shard_map/jit(cholesky)/cholesky | solution.py:61
  686.1 21.1 %custom-call.22 = f32[2,128,128]{1,2,0:T(8,128)} custom-call(f32[2,128,128]{2,1,0:T(8,128)} %get-tuple-element.34), custom_call_target="InvertDiagBlocksLowerTriangular" | custom-call | tf_op jit(solution)/shard_map/jit(_cho_solve)/triangular_solve | solution.py:63
  712.7 13.6 %fusion.2 = f32[256,12288]{1,0:T(8,128)S(1)} fusion(f32[256,12288]{1,0:T(8,128)} %copy.126, f32[256,64]{0,1:T(8,128)S(1)} %broadcast_subtract_fusion.2, f32[64,12288]{1,0:T(8,128)S(1)} %get-tuple-element.195, f32[12288]{0:T(1024)} %broadcast_multiply_fusion.10), kind=kOutput, calls=%fused_computation.13 | convolution fusion | flops 2422996992 | bytes 28426240 | tf_op jit(solution)/shard_map/dot_general | solution.py:71
  740.1 135.9 %all-reduce.10.cloned.1.call-done = f32[256,64]{0,1:T(8,128)} async-done(((f32[256,64]{0,1:T(8,128)}), f32[256,64]{0,1:T(8,128)}) %all-reduce.10.cloned.1.call-update) | async-done | bytes 65552 | tf_op jit(solution)/shard_map/psum | solution.py:125
  906.5 12.5 %cholesky.299 = f32[128,128]{1,0:T(8,128)S(1)} custom-call(f32[128,128]{1,0:T(8,128)} %convolution_subtract_fusion.1), custom_call_target="Cholesky" | custom-call | tf_op jit(solution)/shard_map/jit(cholesky)/cholesky | solution.py:61
  929.9 21.1 %custom-call.24 = f32[2,128,128]{1,2,0:T(8,128)} custom-call(f32[2,128,128]{2,1,0:T(8,128)} %get-tuple-element.35), custom_call_target="InvertDiagBlocksLowerTriangular" | custom-call | tf_op jit(solution)/shard_map/jit(_cho_solve)/triangular_solve | solution.py:63
  955.9 13.6 %fusion.1 = f32[256,12288]{1,0:T(8,128)S(1)} fusion(f32[256,12288]{1,0:T(8,128)} %copy.129, f32[256,64]{0,1:T(8,128)S(1)} %broadcast_subtract_fusion.1, f32[64,12288]{1,0:T(8,128)S(1)} %copy-done.1, f32[12288]{0:T(1024)} %broadcast_multiply_fusion.9), kind=kOutput, calls=%fused_computation.11 | convolution fusion | flops 2422996992 | bytes 28426240 | tf_op jit(solution)/shard_map/dot_general | solution.py:71
  982.9 136.2 %all-reduce.12.cloned.1.call-done = f32[256,64]{0,1:T(8,128)} async-done(((f32[256,64]{0,1:T(8,128)}), f32[256,64]{0,1:T(8,128)}) %all-reduce.12.cloned.1.call-update) | async-done | bytes 65552 | tf_op jit(solution)/shard_map/psum | solution.py:125
  1123.8 11.8 cholesky.316
  1149.8 12.5 %cholesky.333 = f32[128,128]{1,0:T(8,128)S(1)} custom-call(f32[128,128]{1,0:T(8,128)} %convolution_subtract_fusion), custom_call_target="Cholesky" | custom-call | tf_op jit(solution)/shard_map/jit(cholesky)/cholesky | solution.py:61
  1173.2 21.1 %custom-call.26 = f32[2,128,128]{1,2,0:T(8,128)} custom-call(f32[2,128,128]{2,1,0:T(8,128)} %get-tuple-element.36), custom_call_target="InvertDiagBlocksLowerTriangular" | custom-call | tf_op jit(solution)/shard_map/jit(_cho_solve)/triangular_solve | solution.py:63
  1199.1 13.4 %fusion = f32[256,12288]{1,0:T(8,128)S(1)} fusion(f32[256,12288]{1,0:T(8,128)} %copy.132, f32[256,64]{0,1:T(8,128)S(1)} %broadcast_subtract_fusion, f32[64,12288]{1,0:T(8,128)S(1)} %copy-done.5, f32[12288]{0:T(1024)} %broadcast_multiply_fusion.8), kind=kOutput, calls=%fused_computation.9 | convolution fusion | flops 2422996992 | bytes 28426240 | tf_op jit(solution)/shard_map/dot_general | solution.py:71
  (315 shorter events, 389.6 us)
Async XLA Ops:
  10.9 7.9 collective-permute-start
  12.3 6.5 collective-permute-start.1
  24.7 3.4 collective-permute-start.2
  26.0 3.7 collective-permute-start.3
  31.8 4.7 collective-permute-start.4
  35.6 1.2 collective-permute-start.5
  40.0 4.2 collective-permute-start.6
  43.4 1.2 collective-permute-start.7
  46.3 4.2 collective-permute-start.8
  49.7 1.2 collective-permute-start.9
  54.2 4.2 collective-permute-start.10
  57.5 1.2 collective-permute-start.11
  60.5 4.2 collective-permute-start.12
  63.8 1.2 collective-permute-start.13
  68.2 4.2 collective-permute-start.14
  71.6 1.2 collective-permute-start.15
  99.0 103.7 %all-to-all-start = ((f32[16,1,49152]{2,1,0:T(1,128)}), f32[16,1,49152]{2,1,0:T(1,128)S(1)}, u32[]{:S(2)}, u32[]{:S(2)}) async-start(f32[16,1,49152]{2,1,0:T(1,128)} %reshape.856), calls=%async_computation | async-start | bytes 6291456 | tf_op jit(solution)/shard_map/all_to_all | solution.py:87
  106.6 282.0 %all-reduce.6.cloned.1.call-start = ((), (), s32[]{:S(2)}) async-start(), calls=%async_computation.1 | async-start | bytes 131072 | tf_op jit(solution)/shard_map/psum | solution.py:125
  243.5 225.8 %copy-start.2 = (f32[64,12288]{1,0:T(8,128)}, f32[64,12288]{1,0:T(8,128)S(1)}, u32[]{:S(2)}) copy-start(f32[64,12288]{1,0:T(8,128)S(1)} %reshape.826) | copy-start | bytes 9437188
  246.7 385.8 %all-reduce.8.cloned.1.call-start = ((), (), s32[]{:S(2)}) async-start(), calls=%async_computation.2 | async-start | bytes 131072 | tf_op jit(solution)/shard_map/psum | solution.py:125
  495.7 380.3 %all-reduce.10.cloned.1.call-start = ((), (), s32[]{:S(2)}) async-start(), calls=%async_computation.3 | async-start | bytes 131072 | tf_op jit(solution)/shard_map/psum | solution.py:125
  739.2 216.7 %copy-start.1 = (f32[64,12288]{1,0:T(8,128)S(1)}, f32[64,12288]{1,0:T(8,128)}, u32[]{:S(2)}) copy-start(f32[64,12288]{1,0:T(8,128)} %copy-done) | copy-start | bytes 9437188
  739.2 379.9 %all-reduce.12.cloned.1.call-start = ((), (), s32[]{:S(2)}) async-start(), calls=%async_computation.4 | async-start | bytes 131072 | tf_op jit(solution)/shard_map/psum | solution.py:125
  982.3 216.8 %copy-start.5 = (f32[64,12288]{1,0:T(8,128)S(1)}, f32[64,12288]{1,0:T(8,128)}, u32[]{:S(2)}) copy-start(f32[64,12288]{1,0:T(8,128)} %copy-done.4) | copy-start | bytes 9437188
  (33 other events, 445.2 us)
Sparse Core Ops, SparseCore 0:
  246.8 141.7 all-reduce.5
  495.8 136.6 all-reduce.7
  739.3 136.6 all-reduce.9
  982.4 136.6 all-reduce.11
where the time goes:
time: 1240 us; the launch traced here: 1230 us
  waiting for transfers between devices  559 us (45%)
  other arithmetic  300 us (24%)
  local copies, waits for them, and re-layouts  185 us (15%)
  matrix products  132 us (11%)
  starting transfers between devices  33.5 us (3%)
  between operations  19.3 us (2%)
    psum x4, waiting for transfers between devices, local(): prior_obs = lax.psum(local_part, ('mem', 'sub'))  549 us
    another operation x27, other arithmetic, analysis_weights(): factor = jnp.linalg.cholesky(innov_cov)  148 us
    another operation x9, other arithmetic, analysis_weights(): solved = jax.scipy.linalg.cho_solve((factor, True), right_side)  88.9 us
    mul x8, local copies, waits for them, and re-layouts, update_state(): cross_cov.reshape(obs_count, 3, cell_count) * loc_weight[:, None, :]  79.6 us
    dot_general x4, matrix products, update_state(): jnp.dot(obs_anom, state_anom, precision=highest) / (member_count - 1)  54.3 us
    unnamed x76, local copies, waits for them, and re-layouts  41 us
    dot_general x4, matrix products, update_state(): return members + jnp.dot(weights_mix.T, loc_gain, precision=highest)  33.4 us
    another operation x29, local copies, waits for them, and re-layouts, analysis_weights(): solved = jax.scipy.linalg.cho_solve((factor, True), right_side)  27.8 us
  transfers between devices with their start and end apart: 21, of which 18 were waited for; matrix products, arithmetic and copies ran while one was open for 8% of the time, Pallas kernels for 0%

commit v1 on v0

--- a/solution.py
+++ b/solution.py
@@ -122,7 +122,7 @@
             (((1,), (1,)), ((), ())),
             precision=highest,
         )
-        prior_obs = lax.psum(local_part, ("mem", "sub"))
+        prior_obs = jnp.sum(lax.all_gather(local_part, ("mem", "sub")), axis=0)
         obs_anom, weights_mix = analysis_weights(prior_obs, obs_value[batch_id], obs_var[batch_id])
         loc_weight = localize(obs_x, obs_y, cell_x, cell_y, radius_sq, size_x, size_y)
         members = update_state(members, obs_anom, weights_mix, loc_weight, cell_count)

time: 1240 us -> 961 us (0.78)
  waiting for transfers between devices: 559 us -> 241 us
  local copies, waits for them, and re-layouts: 185 us -> 205 us
  other arithmetic: 300 us -> 316 us
    psum x4 -> x0, waiting for transfers between devices: 549 us -> none  [local(): prior_obs = lax.psum(local_part, ('mem', 'sub'))]
    all_gather x0 -> x4, waiting for transfers between devices: none -> 195 us  [local(): prior_obs = jnp.sum(lax.all_gather(local_part, ('mem', 'sub')), axis=0)]
    all_to_all x1, waiting for transfers between devices: 0.01 us -> 37.6 us  [local(): lax.all_to_all(jnp.stack([height, east_wind, north_wind], 1), 'mem', spli...]
    unnamed x76 -> x66, local copies, waits for them, and re-layouts: 41 us -> 61.3 us
    reduce_sum x4 -> x8, other arithmetic: 3.45 us -> 16.1 us  [analysis_weights(): obs_mean = jnp.mean(prior_obs, 1)]
  transfers between devices with their start and end apart: 21 -> 21, of which waited for: 18 -> 21; matrix products, arithmetic and copies ran while one was open for 8% -> 11% of each run, Pallas kernels for 0% -> 0%
where the time goes in v1:
time: 961 us; the launch traced here: 949 us
  other arithmetic  316 us (33%)
  waiting for transfers between devices  241 us (25%)
  local copies, waits for them, and re-layouts  205 us (21%)
  matrix products  133 us (14%)
  starting transfers between devices  34.9 us (4%)
  between operations  19.2 us (2%)
    all_gather x4, waiting for transfers between devices, local(): prior_obs = jnp.sum(lax.all_gather(local_part, ('mem', 'sub')), axis=0)  195 us
    another operation x27, other arithmetic, analysis_weights(): factor = jnp.linalg.cholesky(innov_cov)  150 us
    another operation x9, other arithmetic, analysis_weights(): solved = jax.scipy.linalg.cho_solve((factor, True), right_side)  88.9 us
    mul x8, local copies, waits for them, and re-layouts, update_state(): cross_cov.reshape(obs_count, 3, cell_count) * loc_weight[:, None, :]  79.2 us
    unnamed x66, local copies, waits for them, and re-layouts  61.3 us
    dot_general x4, matrix products, update_state(): jnp.dot(obs_anom, state_anom, precision=highest) / (member_count - 1)  53.1 us
    all_to_all x1, waiting for transfers between devices, local(): lax.all_to_all(jnp.stack([height, east_wind, north_wind], 1), 'mem', spli...  37.6 us
    dot_general x4, matrix products, update_state(): return members + jnp.dot(weights_mix.T, loc_gain, precision=highest)  35.1 us
  transfers between devices with their start and end apart: 21, of which 21 were waited for; matrix products, arithmetic and copies ran while one was open for 11% of the time, Pallas kernels for 0%

profile of v1, /device:TPU:1, one launch (start us, length us, event | category | flops | bytes accessed | tf_op | source)
XLA Modules:
  0.0 948.9 jit_solution(3183924278917942165)
XLA Ops:
  77.5 15.4 %reshape.864 = f32[16,1,49152]{2,1,0:T(1,128)} reshape(f32[2048,3,4,32]{3,2,1,0:T(4,128)} %bitcast.251) | data formatting | bytes 6291456
  100.9 37.6 %all-to-all-done = f32[16,1,49152]{2,1,0:T(1,128)S(1)} async-done(((f32[16,1,49152]{2,1,0:T(1,128)}), f32[16,1,49152]{2,1,0:T(1,128)S(1)}, u32[]{:S(2)}, u32[]{:S(2)}) %all-to-all-start) | async-done | bytes 3145760 | tf_op jit(solution)/shard_map/all_to_all | solution.py:87
  149.7 14.9 %reshape.865 = f32[2048,3,4,32]{3,2,1,0:T(4,128)} reshape(f32[16,49152]{1,0:T(8,128)} %reduce.21) | data formatting | bytes 6291456
  183.3 14.0 %fusion.34 = (f32[256,4096]{0,1:T(8,128)}, f32[256,4096]{0,1:T(8,128)}, f32[256,4096]{0,1:T(8,128)}, f32[256,4096]{0,1:T(8,128)S(1)}) fusion(s32[256]{0:T(256)S(1)} %get-tuple-element.71, s32[256]{0:T(256)S(1)} %get-tuple-element.70, f32[4096]{0:T(1024)S(1)} %multiply_bitcast_fusion, s32[4096]{0:T(1024)S(1)} %get-tuple-element.210, ...), kind=kLoop, calls=%fused_computation.62 | loop fusion | flops 67108864 | bytes 16834560 | tf_op jit(solution)/shard_map/square | solution.py:51
  202.8 12.6 %copy.127 = f32[256,12288]{1,0:T(8,128)} copy(f32[256,12288]{0,1:T(8,128)} %bitcast.247) | data formatting | bytes 25165824 | tf_op jit(solution)/shard_map/mul | solution.py:72
  219.8 39.3 %all-gather.9.cloned.1.call-done = f32[32768,64]{0,1:T(8,128)} async-done(((f32[256,64]{0,1:T(8,128)}), f32[32768,64]{0,1:T(8,128)}) %all-gather.9.cloned.1.call-update) | async-done | bytes 8388624 | tf_op jit(solution)/shard_map/all_gather | solution.py:125
  300.4 12.7 %cholesky.231 = f32[128,128]{1,0:T(8,128)S(1)} custom-call(f32[128,128]{1,0:T(8,128)} %convolution_subtract_fusion.3), custom_call_target="Cholesky" | custom-call | tf_op jit(solution)/shard_map/jit(cholesky)/cholesky | solution.py:61
  323.4 21.1 %custom-call.20 = f32[2,128,128]{1,2,0:T(8,128)} custom-call(f32[2,128,128]{2,1,0:T(8,128)} %get-tuple-element.33), custom_call_target="InvertDiagBlocksLowerTriangular" | custom-call | tf_op jit(solution)/shard_map/jit(_cho_solve)/triangular_solve | solution.py:63
  350.0 13.2 %fusion.3 = f32[256,12288]{1,0:T(8,128)S(1)} fusion(f32[256,12288]{1,0:T(8,128)} %copy.127, f32[256,64]{0,1:T(8,128)S(1)} %broadcast_subtract_fusion.3, f32[64,12288]{1,0:T(8,128)S(1)} %reshape.826, f32[12288]{0:T(1024)} %bitcast.264), kind=kOutput, calls=%fused_computation.15 | convolution fusion | flops 2422996992 | bytes 28426240 | tf_op jit(solution)/shard_map/dot_general | solution.py:71
  383.8 12.6 %copy.130 = f32[256,12288]{1,0:T(8,128)} copy(f32[256,12288]{0,1:T(8,128)} %bitcast.248) | data formatting | bytes 25165824 | tf_op jit(solution)/shard_map/mul | solution.py:72
  397.6 51.6 %all-gather.11.cloned.1.call-done = f32[32768,64]{0,1:T(8,128)} async-done(((f32[256,64]{0,1:T(8,128)}), f32[32768,64]{0,1:T(8,128)}) %all-gather.11.cloned.1.call-update) | async-done | bytes 8388624 | tf_op jit(solution)/shard_map/all_gather | solution.py:125
  490.4 12.7 %cholesky.265 = f32[128,128]{1,0:T(8,128)S(1)} custom-call(f32[128,128]{1,0:T(8,128)} %convolution_subtract_fusion.2), custom_call_target="Cholesky" | custom-call | tf_op jit(solution)/shard_map/jit(cholesky)/cholesky | solution.py:61
  514.0 21.1 %custom-call.22 = f32[2,128,128]{1,2,0:T(8,128)} custom-call(f32[2,128,128]{2,1,0:T(8,128)} %get-tuple-element.34), custom_call_target="InvertDiagBlocksLowerTriangular" | custom-call | tf_op jit(solution)/shard_map/jit(_cho_solve)/triangular_solve | solution.py:63
  540.0 13.2 %fusion.2 = f32[256,12288]{1,0:T(8,128)S(1)} fusion(f32[256,12288]{1,0:T(8,128)} %copy.130, f32[256,64]{0,1:T(8,128)S(1)} %broadcast_subtract_fusion.2, f32[64,12288]{1,0:T(8,128)S(1)} %get-tuple-element.195, f32[12288]{0:T(1024)} %broadcast_multiply_fusion.10), kind=kOutput, calls=%fused_computation.13 | convolution fusion | flops 2422996992 | bytes 28426240 | tf_op jit(solution)/shard_map/dot_general | solution.py:71
  573.8 12.6 %copy.133 = f32[256,12288]{1,0:T(8,128)} copy(f32[256,12288]{0,1:T(8,128)} %bitcast.249) | data formatting | bytes 25165824 | tf_op jit(solution)/shard_map/mul | solution.py:72
  587.6 51.6 %all-gather.13.cloned.1.call-done = f32[32768,64]{0,1:T(8,128)} async-done(((f32[256,64]{0,1:T(8,128)}), f32[32768,64]{0,1:T(8,128)}) %all-gather.13.cloned.1.call-update) | async-done | bytes 8388624 | tf_op jit(solution)/shard_map/all_gather | solution.py:125
  679.9 12.7 %cholesky.299 = f32[128,128]{1,0:T(8,128)S(1)} custom-call(f32[128,128]{1,0:T(8,128)} %convolution_subtract_fusion.1), custom_call_target="Cholesky" | custom-call | tf_op jit(solution)/shard_map/jit(cholesky)/cholesky | solution.py:61
  703.1 21.1 %custom-call.24 = f32[2,128,128]{1,2,0:T(8,128)} custom-call(f32[2,128,128]{2,1,0:T(8,128)} %get-tuple-element.35), custom_call_target="InvertDiagBlocksLowerTriangular" | custom-call | tf_op jit(solution)/shard_map/jit(_cho_solve)/triangular_solve | solution.py:63
  729.1 13.2 %fusion.1 = f32[256,12288]{1,0:T(8,128)S(1)} fusion(f32[256,12288]{1,0:T(8,128)} %copy.133, f32[256,64]{0,1:T(8,128)S(1)} %broadcast_subtract_fusion.1, f32[64,12288]{1,0:T(8,128)S(1)} %get-tuple-element.199, f32[12288]{0:T(1024)} %broadcast_multiply_fusion.9), kind=kOutput, calls=%fused_computation.11 | convolution fusion | flops 2422996992 | bytes 28426240 | tf_op jit(solution)/shard_map/dot_general | solution.py:71
  762.8 12.6 %copy.136 = f32[256,12288]{1,0:T(8,128)} copy(f32[256,12288]{0,1:T(8,128)} %bitcast.250) | data formatting | bytes 25165824 | tf_op jit(solution)/shard_map/mul | solution.py:72
  776.1 52.2 %all-gather.15.cloned.1.call-done = f32[32768,64]{0,1:T(8,128)} async-done(((f32[256,64]{0,1:T(8,128)}), f32[32768,64]{0,1:T(8,128)}) %all-gather.15.cloned.1.call-update) | async-done | bytes 8388624 | tf_op jit(solution)/shard_map/all_gather | solution.py:125
  869.0 12.7 %cholesky.333 = f32[128,128]{1,0:T(8,128)S(1)} custom-call(f32[128,128]{1,0:T(8,128)} %convolution_subtract_fusion), custom_call_target="Cholesky" | custom-call | tf_op jit(solution)/shard_map/jit(cholesky)/cholesky | solution.py:61
  892.6 21.1 %custom-call.26 = f32[2,128,128]{1,2,0:T(8,128)} custom-call(f32[2,128,128]{2,1,0:T(8,128)} %get-tuple-element.36), custom_call_target="InvertDiagBlocksLowerTriangular" | custom-call | tf_op jit(solution)/shard_map/jit(_cho_solve)/triangular_solve | solution.py:63
  918.6 13.4 %fusion = f32[256,12288]{1,0:T(8,128)S(1)} fusion(f32[256,12288]{1,0:T(8,128)} %copy.136, f32[256,64]{0,1:T(8,128)S(1)} %broadcast_subtract_fusion, f32[64,12288]{1,0:T(8,128)S(1)} %copy-done.3, f32[12288]{0:T(1024)} %broadcast_multiply_fusion.8), kind=kOutput, calls=%fused_computation.9 | convolution fusion | flops 2422996992 | bytes 28426240 | tf_op jit(solution)/shard_map/dot_general | solution.py:71
  (317 shorter events, 438.9 us)
Async XLA Ops:
  9.5 4.3 collective-permute-start
  10.8 3.3 collective-permute-start.1
  18.6 4.7 collective-permute-start.2
  22.4 1.2 collective-permute-start.3
  25.7 4.2 collective-permute-start.4
  29.1 1.2 collective-permute-start.5
  33.5 4.2 collective-permute-start.6
  36.8 1.2 collective-permute-start.7
  39.8 4.2 collective-permute-start.8
  43.2 1.2 collective-permute-start.9
  48.0 4.2 collective-permute-start.10
  51.4 1.2 collective-permute-start.11
  54.3 4.2 collective-permute-start.12
  57.7 1.2 collective-permute-start.13
  62.0 4.2 collective-permute-start.14
  65.4 1.2 collective-permute-start.15
  92.9 45.6 %all-to-all-start = ((f32[16,1,49152]{2,1,0:T(1,128)}), f32[16,1,49152]{2,1,0:T(1,128)S(1)}, u32[]{:S(2)}, u32[]{:S(2)}) async-start(f32[16,1,49152]{2,1,0:T(1,128)} %reshape.864), calls=%async_computation | async-start | bytes 6291456 | tf_op jit(solution)/shard_map/all_to_all | solution.py:87
  100.6 158.6 %all-gather.9.cloned.1.call-start = ((), (), s32[]{:S(2)}) async-start(), calls=%async_computation.1 | async-start | bytes 8454144 | tf_op jit(solution)/shard_map/all_gather | solution.py:125
  178.9 171.1 %copy-start.1 = (f32[64,12288]{1,0:T(8,128)}, f32[64,12288]{1,0:T(8,128)S(1)}, u32[]{:S(2)}) copy-start(f32[64,12288]{1,0:T(8,128)S(1)} %reshape.826) | copy-start | bytes 9437188
  182.1 267.1 %all-gather.11.cloned.1.call-start = ((), (), s32[]{:S(2)}) async-start(), calls=%async_computation.2 | async-start | bytes 8454144 | tf_op jit(solution)/shard_map/all_gather | solution.py:125
  372.8 167.2 %copy-start = (f32[64,12288]{1,0:T(8,128)}, f32[64,12288]{1,0:T(8,128)S(1)}, u32[]{:S(2)}) copy-start(f32[64,12288]{1,0:T(8,128)S(1)} %get-tuple-element.195) | copy-start | bytes 9437188
  376.0 263.2 %all-gather.13.cloned.1.call-start = ((), (), s32[]{:S(2)}) async-start(), calls=%async_computation.3 | async-start | bytes 8454144 | tf_op jit(solution)/shard_map/all_gather | solution.py:125
  566.0 262.3 %all-gather.15.cloned.1.call-start = ((), (), s32[]{:S(2)}) async-start(), calls=%async_computation.4 | async-start | bytes 8454144 | tf_op jit(solution)/shard_map/all_gather | solution.py:125
  840.1 78.5 %copy-start.3 = (f32[64,12288]{1,0:T(8,128)S(1)}, f32[64,12288]{1,0:T(8,128)}, u32[]{:S(2)}) copy-start(f32[64,12288]{1,0:T(8,128)} %copy-done.2) | copy-start | bytes 9437188
  (26 other events, 260.2 us)
Sparse Core Ops, SparseCore 0:
  182.2 76.9 all-gather.8
  376.1 73.0 all-gather.10
  566.1 73.0 all-gather.12
  755.2 73.0 all-gather.14
